TPU v7x, 512 devices: a whole 4x8x8 slice. The times are simulated.
512 devices in a mesh: region: 32 (over x, z), batch: 16 (over y, core).
Axes of the slice: x: 4, y: 8, z: 8, core: 2. Of those that a mesh axis runs over, the one named last changes fastest.
Arguments:
- basis_values: bfloat16 [128, 2, 4096, 512], P('region', None, 'batch'), may hold values from -6 to 6
- dens_tiles: bfloat16 [128, 512, 512], P('region', 'batch'), may hold values from -0.005859375 to 0.005859375
- region_tiles: int32 [128, 3], replicated, may hold values from 0 to 127, as said below
- point_counts: int32 [128, 16], P('region', 'batch'), may hold values from 64 to 256, as said below
- point_weights: float32 [128, 4096], P('region', 'batch'), may hold values from 0.0078125 to 0.03125
Outputs:
- xc_tiles: float32 [128, 512, 512], P('region', 'batch')
Inputs may be any that keep to these rules, and one draw needn't show every extreme that they name: `region_tiles`: tile t is stored on index t // 4 of region. Regions 4 * i to 4 * i + 3 lie on index i; among their 12 entries no owner index holds more than 1 and some owner holds exactly 1, on every index; the entries of one owner on one index are different tiles. `point_counts`: every region has at least one batch with all 256 points live.
All inputs are finite; a program needn't handle non-finite values.
Results may differ from a plain program's by a relative error of at most 0.004.
Values may be sent and summed in bfloat16 or wider, within the bound.
A program may use at most 64 MiB of HBM per device.

v0:
```python
import jax
import jax.numpy as jnp
from jax import lax
from jax.sharding import PartitionSpec as P

SLATER = 0.9847450218426964


def potential(density):
    return -SLATER * density * jnp.power(density * density + 1.0, -1.0 / 3.0)


def shards(basis_values, dens_tiles, region_tiles, point_counts, point_weights):
    owner_count = lax.axis_size("region")
    batch_count = lax.axis_size("batch")
    my_index = lax.axis_index("region")
    region_local = basis_values.shape[0]
    point_local = basis_values.shape[2]
    tile_local = dens_tiles.shape[0]
    row_count = dens_tiles.shape[1]
    block_width = dens_tiles.shape[2]
    requests = 3 * region_local
    slot_total = (requests + owner_count - 1) // owner_count
    table = region_tiles.reshape(owner_count, requests)
    owners = table // tile_local
    local_ids = table % tile_local
    order = jnp.arange(requests, dtype=jnp.int32)
    earlier = (owners[:, :, None] == owners[:, None, :]) & (
        order[None, None, :] < order[None, :, None]
    )
    ranks = jnp.sum(earlier.astype(jnp.int32), axis=2)
    slot_ids = jnp.arange(slot_total, dtype=jnp.int32)
    tile_ids = jnp.arange(tile_local, dtype=jnp.int32)
    chosen = (
        (owners == my_index)[:, :, None, None]
        & (ranks[:, :, None, None] == slot_ids[None, None, :, None])
        & (local_ids[:, :, None, None] == tile_ids[None, None, None, :])
    )
    selector = jnp.sum(chosen.astype(jnp.float32), axis=1)
    my_owners = lax.dynamic_index_in_dim(owners, my_index, 0, keepdims=False)
    my_ranks = lax.dynamic_index_in_dim(ranks, my_index, 0, keepdims=False)
    outgoing = jnp.einsum(
        "dct,trb->dcrb",
        selector.astype(jnp.bfloat16),
        dens_tiles,
        preferred_element_type=jnp.float32,
    ).astype(jnp.bfloat16)
    incoming = lax.all_to_all(outgoing, "region", split_axis=0, concat_axis=0, tiled=True)
    flat = incoming.reshape(owner_count * slot_total, row_count, block_width)
    fetched = jnp.take(flat, my_owners * slot_total + my_ranks, axis=0)
    piece = lax.all_gather(fetched, "batch", axis=1, tiled=True)
    count = piece.shape[1]
    shaped = piece.reshape(region_local, 3, count, block_width)
    left_aa = jnp.einsum(
        "rpc,rcb->rpb", basis_values[:, 0], shaped[:, 0], preferred_element_type=jnp.float32
    )
    left_ab = jnp.einsum(
        "rpc,rcb->rpb", basis_values[:, 0], shaped[:, 1], preferred_element_type=jnp.float32
    )
    left_bb = jnp.einsum(
        "rpc,rcb->rpb", basis_values[:, 1], shaped[:, 2], preferred_element_type=jnp.float32
    )
    left_aa, left_ab, left_bb = (left_aa, left_ab, left_bb)
    phi_a = basis_values[:, 0]
    phi_b = basis_values[:, 1]
    density = (
        jnp.sum(phi_a * left_aa, axis=-1)
        + 2.0 * jnp.sum(phi_b * left_ab, axis=-1)
        + jnp.sum(phi_b * left_bb, axis=-1)
    )
    live = jnp.arange(point_local, dtype=jnp.int32)[None, :] < point_counts
    scale = jnp.where(live, point_weights * potential(density), 0.0)
    scaled_a = (scale[:, :, None] * phi_a).astype(jnp.bfloat16)
    scaled_b = (scale[:, :, None] * phi_b).astype(jnp.bfloat16)
    first = jnp.einsum("rpc,rpb->crb", phi_a, scaled_a, preferred_element_type=jnp.float32)
    second = jnp.einsum("rpc,rpb->crb", phi_a, scaled_b, preferred_element_type=jnp.float32)
    third = jnp.einsum("rpc,rpb->crb", phi_b, scaled_b, preferred_element_type=jnp.float32)
    partial_pairs = jnp.stack([first, second, third], axis=2).reshape(
        block_width, requests, block_width
    )
    partial_pairs = partial_pairs.astype(jnp.bfloat16).reshape(
        batch_count, row_count, requests, block_width
    )
    received = lax.all_to_all(partial_pairs, "batch", split_axis=0, concat_axis=0, tiled=True)
    pairs = jnp.sum(received.astype(jnp.float32), axis=0)
    placement = (
        (my_owners[:, None, None] == jnp.arange(owner_count, dtype=jnp.int32)[None, :, None])
        & (my_ranks[:, None, None] == slot_ids[None, None, :])
    ).astype(jnp.float32)
    outgoing_sums = jnp.einsum("jdc,rjb->dcrb", placement, pairs, precision=lax.Precision.HIGHEST)
    returned = lax.all_to_all(outgoing_sums, "region", split_axis=0, concat_axis=0, tiled=True)
    return jnp.einsum("dct,dcrb->trb", selector, returned, precision=lax.Precision.HIGHEST)


def solution(mesh):
    return jax.shard_map(
        shards,
        mesh=mesh,
        in_specs=(
            P("region", None, "batch", None),
            P("region", "batch", None),
            P(),
            P("region", "batch"),
            P("region", "batch"),
        ),
        out_specs=P("region", "batch", None),
        check_vma=False,
    )
```

profile of v0, /device:TPU:1, one launch (start us, length us, event | category | flops | bytes accessed | tf_op | source)
XLA Modules:
  0.0 331.1 jit_solution(2894611914320594194)
XLA Ops:
  6.5 0.8 copy.81
  7.4 0.1 reshape.254
  7.4 0.1 copy.82
  7.6 0.1 convert_reduce_fusion.1
  7.7 0.5 fusion.14
  8.2 1.6 copy.88
  9.8 13.8 %all-to-all-start = ((bf16[32,1,32,512]{3,2,1,0:T(8,128)(2,1)}), bf16[32,1,32,512]{3,2,1,0:T(8,128)(2,1)S(1)}, u32[]{:S(2)}, u32[]{:S(2)}) async-start(bf16[32,1,32,512]{3,2,1,0:T(8,128)(2,1)} %copy.88), calls=%async_computation | async-start | bytes 2097152 | tf_op jit(solution)/shard_map/all_to_all | solution.py:48
  23.6 0.0 all-gather.2.cloned.1.call-start
  23.7 0.2 dynamic-slice_reduce_fusion
  24.0 24.3 %all-to-all-done = bf16[32,1,32,512]{3,2,1,0:T(8,128)(2,1)S(1)} async-done(((bf16[32,1,32,512]{3,2,1,0:T(8,128)(2,1)}), bf16[32,1,32,512]{3,2,1,0:T(8,128)(2,1)S(1)}, u32[]{:S(2)}, u32[]{:S(2)}) %all-to-all-start) | async-done | bytes 1048608 | tf_op jit(solution)/shard_map/all_to_all | solution.py:48
  48.3 1.4 gather_fusion
  49.6 1.9 broadcast_select_fusion
  51.5 0.0 all-gather.2.cloned.1.call-update
  51.5 49.9 %all-gather.2.cloned.1.call-done = bf16[12,512,512]{2,1,0:T(8,128)(2,1)} async-done(((bf16[12,32,512]{2,1,0:T(8,128)(2,1)}), bf16[12,512,512]{2,1,0:T(8,128)(2,1)}) %all-gather.2.cloned.1.call-update) | async-done | bytes 6291472 | tf_op jit(solution)/shard_map/all_gather | solution.py:51
  101.5 2.5 fusion.2
  104.0 0.9 copy-done.4
  104.9 0.8 fusion
  105.7 0.8 fusion.3
  106.5 0.1 multiply_select_fusion
  106.6 0.9 convert_bitcast_fusion.1
  107.5 0.9 convert_bitcast_fusion
  108.4 0.9 convert_bitcast_fusion.2
  109.4 0.8 pad_maximum_fusion
  110.2 0.4 copy.99
  110.6 1.1 copy.100
  111.8 145.4 %all_to_all.15 = bf16[16,32,12,512]{3,1,2,0:T(8,128)(2,1)S(1)} all-to-all(bf16[16,32,12,512]{3,1,2,0:T(8,128)(2,1)S(1)} %copy.100), channel_id=1, replica_groups=mesh['region'=32,'batch'=16] {'batch'}, dimensions={0} | all-to-all | bytes 12582912 | tf_op jit(solution)/shard_map/all_to_all | solution.py:84
  257.1 1.3 convert_reduce_fusion
  258.4 1.4 convolution_bitcast_fusion
  259.8 1.2 copy.103
  261.0 60.3 %all_to_all.16 = f32[32,1,32,512]{3,2,1,0:T(8,128)S(1)} all-to-all(f32[32,1,32,512]{3,2,1,0:T(8,128)S(1)} %copy.103), channel_id=1, replica_groups=mesh['region'=32,'batch'=16] {'region'}, dimensions={0} | all-to-all | bytes 4194304 | tf_op jit(solution)/shard_map/all_to_all | solution.py:91
  321.3 2.2 fusion.8
  323.5 0.8 copy.105
  (16 shorter events, 0.1 us)
Async XLA Ops:
  6.5 1.2 copy-start
  9.8 91.7 %copy-start.1 = (bf16[4,2,256,512]{3,2,1,0:T(8,128)(2,1)S(1)}, bf16[4,2,256,512]{3,2,1,0:T(8,128)(2,1)}, u32[]{:S(2)}) copy-start(bf16[4,2,256,512]{3,2,1,0:T(8,128)(2,1)} %param.5) | copy-start | bytes 6291460
  9.8 38.5 %all-to-all-start = ((bf16[32,1,32,512]{3,2,1,0:T(8,128)(2,1)}), bf16[32,1,32,512]{3,2,1,0:T(8,128)(2,1)S(1)}, u32[]{:S(2)}, u32[]{:S(2)}) async-start(bf16[32,1,32,512]{3,2,1,0:T(8,128)(2,1)} %copy.88), calls=%async_computation | async-start | bytes 2097152 | tf_op jit(solution)/shard_map/all_to_all | solution.py:48
  23.6 77.8 %all-gather.2.cloned.1.call-start = ((), (), s32[]{:S(2)}) async-start(), calls=%async_computation.3 | async-start | bytes 6684672 | tf_op jit(solution)/shard_map/all_gather | solution.py:51
  101.5 3.4 %copy-start.4 = (bf16[12,512,512]{2,1,0:T(8,128)(2,1)S(1)}, bf16[12,512,512]{2,1,0:T(8,128)(2,1)}, u32[]{:S(2)}) copy-start(bf16[12,512,512]{2,1,0:T(8,128)(2,1)} %all-gather.2.cloned.1.call-done) | copy-start | bytes 18874372
  105.7 0.8 copy-start.2
  105.7 0.8 copy-start.3
Sparse Core Ops, SparseCore 0:
  51.6 49.7 all-gather.1
where the time goes:
time: 331 us
  blocking collectives  206 us (62%)
  waiting for transfers between devices  74.3 us (22%)
  starting transfers between devices  13.9 us (4%)
  between operations  13.6 us (4%)
  matrix products  11 us (3%)
  local copies, waits for them, and re-layouts  8.33 us (3%)
  other arithmetic  4.43 us (1%)
    all_to_all x1, blocking collectives, shards(): lax.all_to_all(partial_pairs, 'batch', split_axis=0, concat_axis=0, tiled...  145 us
    all_to_all x1, blocking collectives, shards(): lax.all_to_all(outgoing_sums, 'region', split_axis=0, concat_axis=0, tile...  60.3 us
    all_gather x1, waiting for transfers between devices, shards(): piece = lax.all_gather(fetched, 'batch', axis=1, tiled=True)  49.9 us
    all_to_all x1, waiting for transfers between devices, shards(): lax.all_to_all(outgoing, 'region', split_axis=0, concat_axis=0, tiled=True)  24.3 us
    all_to_all x1, starting transfers between devices, shards(): lax.all_to_all(outgoing, 'region', split_axis=0, concat_axis=0, tiled=True)  13.8 us
  transfers between devices with their start and end apart: 2, of which 2 were waited for; matrix products, arithmetic and copies ran while one was open for 0% of the time, Pallas kernels for 0%

commit v1 on v0

--- a/solution.py
+++ b/solution.py
@@ -48,7 +48,9 @@
     incoming = lax.all_to_all(outgoing, "region", split_axis=0, concat_axis=0, tiled=True)
     flat = incoming.reshape(owner_count * slot_total, row_count, block_width)
     fetched = jnp.take(flat, my_owners * slot_total + my_ranks, axis=0)
-    piece = lax.all_gather(fetched, "batch", axis=1, tiled=True)
+    piece = jnp.concatenate(
+        lax.all_to_all(jnp.stack([fetched] * lax.axis_size("batch")), "batch", 0, 0), axis=1
+    )
     count = piece.shape[1]
     shaped = piece.reshape(region_local, 3, count, block_width)
     left_aa = jnp.einsum(

time: 331 us -> 411 us (1.24)
  blocking collectives: 206 us -> 352 us
  waiting for transfers between devices: 74.3 us -> 24.4 us
  between operations: 13.6 us -> 0.21 us
    all_to_all x0 -> x1, blocking collectives: none -> 153 us  [shards(): lax.all_to_all(jnp.stack([fetched] * lax.axis_size('batch')), 'batch', 0, 0)]
    all_gather x1 -> x0, waiting for transfers between devices: 49.9 us -> none  [shards(): piece = lax.all_gather(fetched, 'batch', axis=1, tiled=True)]
    all_to_all x1, blocking collectives: 60.3 us -> 55.2 us  [shards(): lax.all_to_all(outgoing_sums, 'region', split_axis=0, concat_axis=0, tile...]
  transfers between devices with their start and end apart: 2 -> 1, of which waited for: 2 -> 1; matrix products, arithmetic and copies ran while one was open for 0% -> 0% of each run, Pallas kernels for 0% -> 0%
where the time goes in v1:
time: 411 us
  blocking collectives  352 us (86%)
  waiting for transfers between devices  24.4 us (6%)
  starting transfers between devices  13.7 us (3%)
  matrix products  9.29 us (2%)
  local copies, waits for them, and re-layouts  9.03 us (2%)
    all_to_all x1, blocking collectives, shards(): lax.all_to_all(jnp.stack([fetched] * lax.axis_size('batch')), 'batch', 0, 0)  153 us
    all_to_all x1, blocking collectives, shards(): lax.all_to_all(partial_pairs, 'batch', split_axis=0, concat_axis=0, tiled...  144 us
    all_to_all x1, blocking collectives, shards(): lax.all_to_all(outgoing_sums, 'region', split_axis=0, concat_axis=0, tile...  55.2 us
    all_to_all x1, waiting for transfers between devices, shards(): lax.all_to_all(outgoing, 'region', split_axis=0, concat_axis=0, tiled=True)  24.4 us
    all_to_all x1, starting transfers between devices, shards(): lax.all_to_all(outgoing, 'region', split_axis=0, concat_axis=0, tiled=True)  13.7 us
  transfers between devices with their start and end apart: 1, of which 1 were waited for; matrix products, arithmetic and copies ran while one was open for 0% of the time, Pallas kernels for 0%

profile of v1, /device:TPU:1, one launch (start us, length us, event | category | flops | bytes accessed | tf_op | source)
XLA Modules:
  0.0 410.8 jit_solution(12873191094888985087)
XLA Ops:
  0.0 0.8 copy.81
  0.8 0.1 reshape.256
  0.9 0.1 copy.82
  1.0 0.1 convert_reduce_fusion.1
  1.2 0.5 fusion.14
  1.7 1.6 copy.88
  3.3 13.7 %all-to-all-start = ((bf16[32,1,32,512]{3,2,1,0:T(8,128)(2,1)}), bf16[32,1,32,512]{3,2,1,0:T(8,128)(2,1)S(1)}, u32[]{:S(2)}, u32[]{:S(2)}) async-start(bf16[32,1,32,512]{3,2,1,0:T(8,128)(2,1)} %copy.88), calls=%async_computation | async-start | bytes 2097152 | tf_op jit(solution)/shard_map/all_to_all | solution.py:48
  17.0 0.2 dynamic-slice_reduce_fusion
  17.2 24.4 %all-to-all-done = bf16[32,1,32,512]{3,2,1,0:T(8,128)(2,1)S(1)} async-done(((bf16[32,1,32,512]{3,2,1,0:T(8,128)(2,1)}), bf16[32,1,32,512]{3,2,1,0:T(8,128)(2,1)S(1)}, u32[]{:S(2)}, u32[]{:S(2)}) %all-to-all-start) | async-done | bytes 1048608 | tf_op jit(solution)/shard_map/all_to_all | solution.py:48
  41.6 0.6 gather_fusion
  42.2 0.1 broadcast_select_fusion
  42.3 0.8 stack.14
  43.1 152.8 %all_to_all.20 = bf16[16,12,32,512]{3,2,1,0:T(8,128)(2,1)S(1)} all-to-all(bf16[16,12,32,512]{3,2,1,0:T(8,128)(2,1)S(1)} %stack.14), channel_id=1, replica_groups=mesh['region'=32,'batch'=16] {'batch'}, dimensions={0} | all-to-all | bytes 12582912 | tf_op jit(solution)/shard_map/all_to_all | solution.py:52
  195.9 1.1 copy.89
  197.0 0.5 copy-done.1
  197.5 0.8 fusion.2
  198.3 0.8 fusion
  199.1 0.8 fusion.3
  199.9 0.1 multiply_select_fusion
  200.0 0.9 convert_bitcast_fusion.1
  200.9 0.9 convert_bitcast_fusion
  201.8 0.9 convert_bitcast_fusion.2
  202.8 0.8 pad_maximum_fusion
  203.6 0.4 copy.100
  204.0 1.1 copy.101
  205.2 143.6 %all_to_all.21 = bf16[16,32,12,512]{3,1,2,0:T(8,128)(2,1)S(1)} all-to-all(bf16[16,32,12,512]{3,1,2,0:T(8,128)(2,1)S(1)} %copy.101), channel_id=1, replica_groups=mesh['region'=32,'batch'=16] {'batch'}, dimensions={0} | all-to-all | bytes 12582912 | tf_op jit(solution)/shard_map/all_to_all | solution.py:86
  348.8 1.3 convert_reduce_fusion
  350.0 1.4 convolution_bitcast_fusion
  351.4 1.2 copy.104
  352.7 55.2 %all_to_all.22 = f32[32,1,32,512]{3,2,1,0:T(8,128)S(1)} all-to-all(f32[32,1,32,512]{3,2,1,0:T(8,128)S(1)} %copy.104), channel_id=1, replica_groups=mesh['region'=32,'batch'=16] {'region'}, dimensions={0} | all-to-all | bytes 4194304 | tf_op jit(solution)/shard_map/all_to_all | solution.py:93
  407.8 2.2 fusion.8
  410.1 0.8 copy.106
  (14 shorter events, 0.1 us)
Async XLA Ops:
  0.0 1.2 copy-start
  3.3 38.3 %all-to-all-start = ((bf16[32,1,32,512]{3,2,1,0:T(8,128)(2,1)}), bf16[32,1,32,512]{3,2,1,0:T(8,128)(2,1)S(1)}, u32[]{:S(2)}, u32[]{:S(2)}) async-start(bf16[32,1,32,512]{3,2,1,0:T(8,128)(2,1)} %copy.88), calls=%async_computation | async-start | bytes 2097152 | tf_op jit(solution)/shard_map/all_to_all | solution.py:48
  195.9 1.6 copy-start.1
  199.1 0.8 copy-start.2
  199.1 0.8 copy-start.3
